TPU v7x, 32 devices: a whole 2x2x4 slice. The times are simulated.
32 devices in a mesh: rows: 8 (over z, y), cols: 4 (over x, core).
Axes of the slice: x: 2, y: 2, z: 4, core: 2. Of those that a mesh axis runs over, the one named last changes fastest.
Arguments:
- factor: bfloat16 [4096, 256], P(('rows', 'cols')), may hold values from -0.09375 to 0.09375
- cores: bfloat16 [4, 256, 256], replicated, as said below
- tile_values: bfloat16 [4, 96, 512, 128], P(None, 'rows', 'cols'), may hold values from -56 to 56
- tile_rows: int32 [4, 8, 48], P(None, 'rows', 'cols'), may hold values from 0 to 3
- tile_cols: int32 [4, 8, 48], P(None, 'rows', 'cols'), may hold values from 0 to 7
- tile_counts: int32 [4, 8, 4], P(None, 'rows', 'cols'), may hold values from 3 to 12, as said below
Outputs:
- factor_new: bfloat16 [4096, 256], P(('rows', 'cols'))
- cores_new: float32 [4, 256, 256], replicated
Inputs may be any that keep to these rules, and one draw needn't show every extreme that they name: cores are dominated by their positive diagonals. `tile_counts`: every relation has some device whose 12 slots are all used. `tile_rows`: several slots may name the same tile.
All inputs are finite; a program needn't handle non-finite values.
Results may differ from a plain program's by a relative error of at most 0.0034.
The roundings to bfloat16 on the way count: a program that leaves them out, or rounds other values in their place, can miss the bound.
Values may be sent and summed in bfloat16 or wider, within the bound.
No kernel may reach another device: no remote copies, remote signals or barrier semaphores. Data moves between devices by JAX's collectives and lax.ppermute only.
A program may use at most 128 MiB of HBM per device.

v0:
```python
import jax
import jax.numpy as jnp
from jax import lax
from jax.sharding import PartitionSpec as P

ridge_weight = 0.1


def normal_system(summed_gram_matrix, cores_float32):
    direct_part = jnp.einsum(
        "krs,st,kqt->rq",
        cores_float32,
        summed_gram_matrix,
        cores_float32,
        precision=lax.Precision.HIGHEST,
    )
    reflected_part = jnp.einsum(
        "euh,uc,eca->ha",
        cores_float32,
        summed_gram_matrix,
        cores_float32,
        precision=lax.Precision.HIGHEST,
    )
    return (
        direct_part
        + reflected_part
        + ridge_weight * jnp.eye(summed_gram_matrix.shape[0], dtype=jnp.float32)
    )


def solve_rows(cholesky_lhs, numerator):
    halfway = lax.linalg.triangular_solve(cholesky_lhs, numerator.T, left_side=True, lower=True)
    return lax.linalg.triangular_solve(
        cholesky_lhs, halfway, left_side=True, lower=True, transpose_a=True
    ).T


def whiten(cholesky_new, core_num):
    relations, rank_size, _ = core_num.shape
    stacked = core_num.transpose(1, 0, 2).reshape(rank_size, relations * rank_size)
    halfway = lax.linalg.triangular_solve(cholesky_new, stacked, left_side=True, lower=True)
    flipped = (
        halfway.reshape(rank_size, relations, rank_size)
        .transpose(2, 1, 0)
        .reshape(rank_size, relations * rank_size)
    )
    second = lax.linalg.triangular_solve(cholesky_new, flipped, left_side=True, lower=True)
    return second.reshape(rank_size, relations, rank_size).transpose(1, 2, 0)


def local(factor, cores, tile_values, tile_rows, tile_cols, tile_counts):
    relations, slot_count, tile_size, _ = tile_values.shape
    own_rows, rank_size = factor.shape
    row_ids = tile_rows[:, 0, :]
    col_ids = tile_cols[:, 0, :]
    live_mask = (jnp.arange(slot_count, dtype=jnp.int32)[None, :] < tile_counts[:, 0, :]).astype(
        jnp.float32
    )
    cores_float32 = cores.astype(jnp.float32)
    gram_old = lax.psum(
        jnp.dot(factor.T, factor, preferred_element_type=jnp.float32), ("rows", "cols")
    )
    cholesky_lhs = jnp.linalg.cholesky(normal_system(gram_old, cores_float32))
    col_tiles = lax.all_gather(factor, "rows", axis=0, tiled=True).reshape(-1, tile_size, rank_size)
    col_count = col_tiles.shape[0]
    panel_tiles = lax.axis_size("cols") * own_rows // tile_size
    row_partial = jnp.zeros((panel_tiles, tile_size, relations, rank_size), jnp.float32)
    for relation in range(relations):
        products = jnp.einsum(
            "sij,sjr->sir",
            tile_values[relation],
            col_tiles[col_ids[relation]],
            preferred_element_type=jnp.float32,
        )
        products = products * live_mask[relation][:, None, None]
        row_partial = row_partial.at[row_ids[relation], :, relation].add(products)
    row_partial = row_partial.reshape(panel_tiles * tile_size, relations, rank_size)
    flat_partial = row_partial.reshape(panel_tiles * tile_size, relations * rank_size)
    row_sum = lax.psum_scatter(flat_partial, "cols", scatter_dimension=0, tiled=True)
    direct = row_sum.reshape(own_rows, relations, rank_size)
    numerator = jnp.einsum("eks,kqs->eq", direct, cores_float32, precision=lax.Precision.HIGHEST)
    panel = lax.all_gather(factor, "cols", axis=0, tiled=True)
    rotated = jnp.einsum("pr,krs->pks", panel, cores, preferred_element_type=jnp.float32).astype(
        jnp.bfloat16
    )
    rotated_tiles = rotated.reshape(panel_tiles, tile_size, relations, rank_size)
    col_partial = jnp.zeros((col_count, tile_size, rank_size), jnp.float32)
    for relation in range(relations):
        rotated_selection = rotated_tiles[row_ids[relation], :, relation]
        back_products = jnp.einsum(
            "sij,sir->sjr",
            tile_values[relation],
            rotated_selection,
            preferred_element_type=jnp.float32,
        )
        back_products = back_products * live_mask[relation][:, None, None]
        col_partial = col_partial.at[col_ids[relation]].add(back_products)
    col_partial = col_partial.reshape(col_count * tile_size, rank_size)
    numerator = numerator + lax.psum_scatter(col_partial, "rows", scatter_dimension=0, tiled=True)
    factor_new = solve_rows(cholesky_lhs, numerator).astype(jnp.bfloat16)
    gram_part = jnp.dot(factor_new.T, factor_new, preferred_element_type=jnp.float32)
    col_new = lax.all_gather(factor_new, "rows", axis=0, tiled=True).reshape(
        -1, tile_size, rank_size
    )
    panel_new = lax.all_gather(factor_new, "cols", axis=0, tiled=True).reshape(
        -1, tile_size, rank_size
    )
    core_matrices = []
    for relation in range(relations):
        upper = jnp.einsum(
            "sij,sir->sjr",
            tile_values[relation],
            panel_new[row_ids[relation]],
            preferred_element_type=jnp.float32,
        ).astype(jnp.bfloat16)
        upper = jnp.where(live_mask[relation][:, None, None] > 0, upper, jnp.zeros_like(upper))
        core_matrices.append(
            jnp.einsum(
                "sjr,sjq->rq", upper, col_new[col_ids[relation]], preferred_element_type=jnp.float32
            )
        )
    core_part = jnp.stack(core_matrices, axis=0)
    gram_new = lax.psum(gram_part, ("rows", "cols"))
    core_num = lax.psum(core_part, ("rows", "cols"))
    cores_new = whiten(jnp.linalg.cholesky(gram_new), core_num)
    return (factor_new, cores_new)


def solution(mesh):
    in_specs = (
        P(("rows", "cols"), None),
        P(),
        P(None, "rows", "cols", None),
        P(None, "rows", "cols"),
        P(None, "rows", "cols"),
        P(None, "rows", "cols"),
    )
    out_specs = (P(("rows", "cols"), None), P())
    return jax.shard_map(local, mesh=mesh, in_specs=in_specs, out_specs=out_specs, check_vma=False)
```

profile of v0, /device:TPU:0, one launch (start us, length us, event | category | flops | bytes accessed | tf_op | source)
XLA Modules:
  0.0 483.6 jit_solution(10696427226409059928)
XLA Ops:
  8.1 1.9 fusion.113
  10.0 33.4 %all_gather.12 = bf16[1024,256]{1,0:T(8,128)(2,1)S(1)} all-gather(bf16[128,256]{1,0:T(8,128)(2,1)} %param.9), channel_id=1, replica_groups=mesh['rows'=8,'cols'=4] {'rows'}, dimensions={0}, use_global_device_ids=true | all-gather | bytes 589824 | tf_op jit(solution)/shard_map/all_gather | solution.py:64
  50.8 1.8 multiply_bitcast_fusion.7
  52.7 1.6 multiply_bitcast_fusion.6
  54.3 1.6 multiply_bitcast_fusion.5
  55.9 1.6 multiply_bitcast_fusion.4
  57.4 1.6 copy.35
  59.0 3.1 copy.37
  62.2 1.6 copy.39
  63.8 3.0 copy.41
  67.1 3.2 scatter_fusion
  70.2 3.2 scatter_fusion.1
  73.4 3.2 scatter_fusion.2
  76.6 3.2 scatter_fusion.3
  81.1 1.8 copy.97
  83.8 6.0 %all_gather.13 = bf16[512,256]{1,0:T(8,128)(2,1)S(1)} all-gather(bf16[128,256]{1,0:T(8,128)(2,1)S(1)} %copy-done.9), channel_id=1, replica_groups=mesh['rows'=8,'cols'=4] {'cols'}, dimensions={0}, use_global_device_ids=true | all-gather | bytes 327680 | tf_op jit(solution)/shard_map/all_gather | solution.py:82
  90.9 2.7 multiply_bitcast_fusion.3
  93.6 1.9 copy.47
  97.0 2.8 multiply_bitcast_fusion.2
  99.8 3.1 copy.50
  104.5 2.9 multiply_bitcast_fusion.1
  107.4 3.1 copy.53
  111.9 2.8 multiply_bitcast_fusion
  114.7 3.1 copy.56
  117.9 1.8 scatter_fusion.4
  119.8 3.1 scatter_fusion.5
  122.9 1.8 scatter_fusion.6
  124.8 3.1 scatter_fusion.7
  129.5 22.2 %all-reduce.9.cloned.1.call-done = f32[256,256]{1,0:T(8,128)} async-done(((f32[256,256]{1,0:T(8,128)}), f32[256,256]{1,0:T(8,128)}) %all-reduce.9.cloned.1.call-update) | async-done | bytes 262160 | tf_op jit(solution)/shard_map/psum | solution.py:60
  151.7 1.7 fusion.67
  155.7 11.7 %cholesky.130 = f32[128,128]{1,0:T(8,128)S(1)} custom-call(f32[128,128]{1,0:T(8,128)S(1)} %cholesky.194), custom_call_target="Cholesky" | custom-call | tf_op jit(solution)/shard_map/jit(cholesky)/cholesky | solution.py:63
  167.6 9.8 %custom-call.35 = f32[1,128,128]{1,2,0:T(8,128)S(1)} custom-call(f32[1,128,128]{2,1,0:T(8,128)S(1)} %get-tuple-element.75), custom_call_target="InvertDiagBlocksLowerTriangular" | custom-call | tf_op jit(solution)/shard_map/jit(cholesky)/cholesky | solution.py:63
  178.0 11.9 %cholesky.147 = f32[128,128]{1,0:T(8,128)S(1)} custom-call(f32[128,128]{1,0:T(8,128)S(1)} %convolution_subtract_fusion.5), custom_call_target="Cholesky" | custom-call | tf_op jit(solution)/shard_map/jit(cholesky)/cholesky | solution.py:63
  192.2 4.4 while.5
  196.6 19.7 %custom-call.16 = f32[2,128,128]{1,2,0:T(8,128)S(1)} custom-call(f32[2,128,128]{2,1,0:T(8,128)S(1)} %get-tuple-element.19), custom_call_target="InvertDiagBlocksLowerTriangular" | custom-call | tf_op jit(solution)/shard_map/triangular_solve | solution.py:33
  221.5 27.7 %all_gather.15 = bf16[1024,256]{0,1:T(8,128)(2,1)S(1)} all-gather(bf16[128,256]{0,1:T(8,128)(2,1)S(1)} %fusion.88), channel_id=1, replica_groups=mesh['rows'=8,'cols'=4] {'rows'}, dimensions={0}, use_global_device_ids=true | all-gather | bytes 589824 | tf_op jit(solution)/shard_map/all_gather | solution.py:102
  249.2 5.8 %all_gather.14 = bf16[512,256]{0,1:T(8,128)(2,1)S(1)} all-gather(bf16[128,256]{0,1:T(8,128)(2,1)S(1)} %fusion.88), channel_id=1, replica_groups=mesh['rows'=8,'cols'=4] {'cols'}, dimensions={0}, use_global_device_ids=true | all-gather | bytes 327680 | tf_op jit(solution)/shard_map/all_gather | solution.py:105
  266.5 2.1 fusion.12
  268.5 2.1 fusion.13
  270.6 2.8 fusion.14
  273.4 2.5 fusion.15
  275.9 2.1 pad_maximum_fusion
  278.7 128.2 %all-reduce.11.cloned.1.call-done = (f32[256,1024]{0,1:T(8,128)}, f32[256,256]{0,1:T(8,128)}) async-done(((f32[256,1024]{0,1:T(8,128)}, f32[256,256]{0,1:T(8,128)}), (f32[256,1024]{0,1:T(8,128)}, f32[256,256]{0,1:T(8,128)})) %all-reduce.11.cloned.1.call-update) | async-done | bytes 1310736 | tf_op jit(solution)/shard_map/psum | solution.py:124
  409.0 11.7 %cholesky.164 = f32[128,128]{1,0:T(8,128)S(1)} custom-call(f32[128,128]{1,0:T(8,128)S(1)} %cholesky.197), custom_call_target="Cholesky" | custom-call | tf_op jit(solution)/shard_map/jit(cholesky)/cholesky | solution.py:125
  420.8 9.8 %custom-call.36 = f32[1,128,128]{1,2,0:T(8,128)S(1)} custom-call(f32[1,128,128]{2,1,0:T(8,128)S(1)} %get-tuple-element.73), custom_call_target="InvertDiagBlocksLowerTriangular" | custom-call | tf_op jit(solution)/shard_map/jit(cholesky)/cholesky | solution.py:125
  431.1 11.9 %cholesky.181 = f32[128,128]{1,0:T(8,128)S(1)} custom-call(f32[128,128]{1,0:T(8,128)S(1)} %convolution_subtract_fusion.2), custom_call_target="Cholesky" | custom-call | tf_op jit(solution)/shard_map/jit(cholesky)/cholesky | solution.py:125
  445.7 4.1 while.6
  449.8 19.7 %custom-call.38 = f32[2,128,128]{1,2,0:T(8,128)S(1)} custom-call(f32[2,128,128]{2,1,0:T(8,128)S(1)} %get-tuple-element.27), custom_call_target="InvertDiagBlocksLowerTriangular" | custom-call | tf_op jit(solution)/shard_map/triangular_solve/custom-call.5 | solution.py:47
  (140 shorter events, 57.1 us)
Async XLA Ops:
  8.0 81.8 %copy-start = (bf16[4,256,256]{2,1,0:T(8,128)(2,1)S(1)}, bf16[4,256,256]{2,1,0:T(8,128)(2,1)}, u32[]{:S(2)}) copy-start(bf16[4,256,256]{2,1,0:T(8,128)(2,1)} %param.10) | copy-start | bytes 1572868
  8.0 143.7 %all-reduce.9.cloned.1.call-start = ((), (), s32[]{:S(2)}) async-start(), calls=%async_computation.2 | async-start | bytes 524288 | tf_op jit(solution)/shard_map/psum | solution.py:60
  9.9 206.4 %reduce-scatter.3.cloned.1.call-start = ((), (), s32[]{:S(2)}) async-start(), calls=%async_computation.3 | async-start | bytes 2621440 | tf_op jit(solution)/shard_map/reduce_scatter | solution.py:79
  50.7 1.8 copy-start.4
  50.8 2.0 copy-start.6
  52.6 1.7 copy-start.7
  59.0 3.1 copy-start.3
  82.9 0.8 copy-start.9
  82.9 134.6 %reduce-scatter.5.cloned.1.call-start = ((), (), s32[]{:S(2)}) async-start(), calls=%async_computation.4 | async-start | bytes 1179648 | tf_op jit(solution)/shard_map/reduce_scatter | solution.py:99
  119.8 3.1 copy-start.2
  127.9 1.0 copy-start.1
  128.9 278.0 %all-reduce.11.cloned.1.call-start = ((), (), s32[]{:S(2)}) async-start(), calls=%async_computation.5 | async-start | bytes 2621440 | tf_op jit(solution)/shard_map/psum | solution.py:124
  151.7 2.5 copy-start.8
  263.4 3.0 copy-start.5
  409.0 60.6 %copy-start.10 = (f32[256,1024]{0,1:T(8,128)S(1)}, f32[256,1024]{0,1:T(8,128)}, u32[]{:S(2)}) copy-start(f32[256,1024]{0,1:T(8,128)} %get-tuple-element.56) | copy-start | bytes 3145732
Sparse Core Ops, SparseCore 0:
  14.3 137.2 all-reduce.8
  278.1 128.7 all-reduce.10
Sparse Core Ops, SparseCore 1:
  83.0 32.4 reduce-scatter.2
  129.0 64.6 reduce-scatter.4
where the time goes:
time: 492 us; the launch traced here: 484 us
  waiting for transfers between devices  150 us (30%)
  other arithmetic  137 us (28%)
  blocking collectives  72.9 us (15%)
  local copies, waits for them, and re-layouts  61.2 us (12%)
  matrix products  42.5 us (9%)
  between operations  19.3 us (4%)
    psum x1, waiting for transfers between devices, local(): core_num = lax.psum(core_part, ('rows', 'cols'))  128 us
    another operation x7, other arithmetic, local(): cores_new = whiten(jnp.linalg.cholesky(gram_new), core_num)  34.8 us
    another operation x6, other arithmetic, local(): cholesky_lhs = jnp.linalg.cholesky(normal_system(gram_old, cores_float32))  34.2 us
    all_gather x1, blocking collectives, local(): lax.all_gather(factor, 'rows', axis=0, tiled=True)  33.4 us
    all_gather x1, blocking collectives, local(): lax.all_gather(factor_new, 'rows', axis=0, tiled=True)  27.7 us
    psum x1, waiting for transfers between devices, local(): lax.psum(jnp.dot(factor.T, factor, preferred_element_type=jnp.float32), (...  22.2 us
    another operation x3, other arithmetic, whiten(): lax.linalg.triangular_solve(cholesky_new, flipped, left_side=True, lower=...  19.8 us
    another operation x3, other arithmetic, solve_rows(): lax.linalg.triangular_solve(cholesky_lhs, halfway, left_side=True, lower=...  19.7 us
  transfers between devices with their start and end apart: 4, of which 2 were waited for; matrix products, arithmetic and copies ran while one was open for 29% of the time, Pallas kernels for 0%

commit v1 on v0

--- a/solution.py
+++ b/solution.py
@@ -121,7 +121,7 @@
         )
     core_part = jnp.stack(core_matrices, axis=0)
     gram_new = lax.psum(gram_part, ("rows", "cols"))
-    core_num = lax.psum(core_part, ("rows", "cols"))
+    core_num = jax.lax.psum(jax.lax.psum(core_part, axis_name="cols"), axis_name="rows")
     cores_new = whiten(jnp.linalg.cholesky(gram_new), core_num)
     return (factor_new, cores_new)
 

time: 492 us -> 528 us (1.073)
  waiting for transfers between devices: 150 us -> 182 us
    psum x1 -> x3, waiting for transfers between devices: 128 us -> 159 us  [the longest x1 105 us: local(): gram_new = lax.psum(gram_part, ('rows', 'cols'))]
  transfers between devices with their start and end apart: 4 -> 6, of which waited for: 2 -> 4; matrix products, arithmetic and copies ran while one was open for 29% -> 42% of each run, Pallas kernels for 0% -> 0%
where the time goes in v1:
time: 528 us; the launch traced here: 519 us
  waiting for transfers between devices  182 us (34%)
  other arithmetic  136 us (26%)
  blocking collectives  72.9 us (14%)
  local copies, waits for them, and re-layouts  63.7 us (12%)
  matrix products  44.4 us (8%)
  between operations  19.1 us (4%)
    psum x1, waiting for transfers between devices, local(): gram_new = lax.psum(gram_part, ('rows', 'cols'))  105 us
    psum x1, waiting for transfers between devices, local(): jax.lax.psum(jax.lax.psum(core_part, axis_name='cols'), axis_name='rows')  51.4 us
    another operation x7, other arithmetic, local(): cores_new = whiten(jnp.linalg.cholesky(gram_new), core_num)  34.7 us
    another operation x6, other arithmetic, local(): cholesky_lhs = jnp.linalg.cholesky(normal_system(gram_old, cores_float32))  34.2 us
    all_gather x1, blocking collectives, local(): lax.all_gather(factor, 'rows', axis=0, tiled=True)  33.4 us
    all_gather x1, blocking collectives, local(): lax.all_gather(factor_new, 'rows', axis=0, tiled=True)  27.6 us
    psum x1, waiting for transfers between devices, local(): lax.psum(jnp.dot(factor.T, factor, preferred_element_type=jnp.float32), (...  22.2 us
    another operation x3, other arithmetic, whiten(): lax.linalg.triangular_solve(cholesky_new, flipped, left_side=True, lower=...  19.8 us
  transfers between devices with their start and end apart: 6, of which 4 were waited for; matrix products, arithmetic and copies ran while one was open for 42% of the time, Pallas kernels for 0%

profile of v1, /device:TPU:0, one launch (start us, length us, event | category | flops | bytes accessed | tf_op | source)
XLA Modules:
  0.0 519.2 jit_solution(7781579864940370629)
XLA Ops:
  8.1 1.9 fusion.113
  10.0 33.4 %all_gather.12 = bf16[1024,256]{1,0:T(8,128)(2,1)S(1)} all-gather(bf16[128,256]{1,0:T(8,128)(2,1)} %param.9), channel_id=1, replica_groups=mesh['rows'=8,'cols'=4] {'rows'}, dimensions={0}, use_global_device_ids=true | all-gather | bytes 589824 | tf_op jit(solution)/shard_map/all_gather | solution.py:64
  50.8 1.8 multiply_bitcast_fusion.7
  59.0 3.1 copy.37
  63.8 3.0 copy.41
  67.1 3.2 scatter_fusion
  70.2 3.2 scatter_fusion.1
  73.4 3.2 scatter_fusion.2
  76.6 3.2 scatter_fusion.3
  81.1 1.8 copy.90
  83.8 6.0 %all_gather.13 = bf16[512,256]{1,0:T(8,128)(2,1)S(1)} all-gather(bf16[128,256]{1,0:T(8,128)(2,1)S(1)} %copy-done.9), channel_id=1, replica_groups=mesh['rows'=8,'cols'=4] {'cols'}, dimensions={0}, use_global_device_ids=true | all-gather | bytes 327680 | tf_op jit(solution)/shard_map/all_gather | solution.py:82
  90.9 2.6 multiply_bitcast_fusion.3
  93.6 1.9 copy.47
  97.0 2.8 multiply_bitcast_fusion.2
  99.8 3.1 copy.50
  104.5 2.9 multiply_bitcast_fusion.1
  107.3 3.1 copy.53
  111.9 2.8 multiply_bitcast_fusion
  114.7 3.1 copy.56
  117.9 1.8 scatter_fusion.4
  119.8 3.1 scatter_fusion.5
  122.9 1.8 scatter_fusion.6
  124.8 3.1 scatter_fusion.7
  129.4 22.2 %all-reduce.10.cloned.1.call-done = f32[256,256]{1,0:T(8,128)} async-done(((f32[256,256]{1,0:T(8,128)}), f32[256,256]{1,0:T(8,128)}) %all-reduce.10.cloned.1.call-update) | async-done | bytes 262160 | tf_op jit(solution)/shard_map/psum | solution.py:60
  151.7 1.7 fusion.67
  155.7 11.7 %cholesky.130 = f32[128,128]{1,0:T(8,128)S(1)} custom-call(f32[128,128]{1,0:T(8,128)S(1)} %cholesky.194), custom_call_target="Cholesky" | custom-call | tf_op jit(solution)/shard_map/jit(cholesky)/cholesky | solution.py:63
  167.5 9.8 %custom-call.35 = f32[1,128,128]{1,2,0:T(8,128)S(1)} custom-call(f32[1,128,128]{2,1,0:T(8,128)S(1)} %get-tuple-element.73), custom_call_target="InvertDiagBlocksLowerTriangular" | custom-call | tf_op jit(solution)/shard_map/jit(cholesky)/cholesky | solution.py:63
  178.0 11.9 %cholesky.147 = f32[128,128]{1,0:T(8,128)S(1)} custom-call(f32[128,128]{1,0:T(8,128)S(1)} %convolution_subtract_fusion.5), custom_call_target="Cholesky" | custom-call | tf_op jit(solution)/shard_map/jit(cholesky)/cholesky | solution.py:63
  192.2 4.4 while.5
  196.6 19.7 %custom-call.16 = f32[2,128,128]{1,2,0:T(8,128)S(1)} custom-call(f32[2,128,128]{2,1,0:T(8,128)S(1)} %get-tuple-element.19), custom_call_target="InvertDiagBlocksLowerTriangular" | custom-call | tf_op jit(solution)/shard_map/triangular_solve | solution.py:33
  221.5 27.6 %all_gather.15 = bf16[1024,256]{0,1:T(8,128)(2,1)S(1)} all-gather(bf16[128,256]{0,1:T(8,128)(2,1)S(1)} %fusion.88), channel_id=1, replica_groups=mesh['rows'=8,'cols'=4] {'rows'}, dimensions={0}, use_global_device_ids=true | all-gather | bytes 589824 | tf_op jit(solution)/shard_map/all_gather | solution.py:102
  249.1 5.8 %all_gather.14 = bf16[512,256]{0,1:T(8,128)(2,1)S(1)} all-gather(bf16[128,256]{0,1:T(8,128)(2,1)S(1)} %fusion.88), channel_id=1, replica_groups=mesh['rows'=8,'cols'=4] {'cols'}, dimensions={0}, use_global_device_ids=true | all-gather | bytes 327680 | tf_op jit(solution)/shard_map/all_gather | solution.py:105
  267.3 2.0 fusion.12
  269.3 2.0 fusion.13
  271.3 2.7 fusion.14
  274.0 2.5 fusion.15
  276.5 2.1 pad_maximum_fusion
  278.9 104.7 %all-reduce.12.cloned.1.call-done = f32[256,256]{0,1:T(8,128)} async-done(((f32[256,256]{0,1:T(8,128)}), f32[256,256]{0,1:T(8,128)}) %all-reduce.12.cloned.1.call-update) | async-done | bytes 262160 | tf_op jit(solution)/shard_map/psum | solution.py:123
  385.6 11.7 %cholesky.164 = f32[128,128]{1,0:T(8,128)S(1)} custom-call(f32[128,128]{1,0:T(8,128)S(1)} %cholesky.197), custom_call_target="Cholesky" | custom-call | tf_op jit(solution)/shard_map/jit(cholesky)/cholesky | solution.py:125
  397.4 9.8 %custom-call.36 = f32[1,128,128]{1,2,0:T(8,128)S(1)} custom-call(f32[1,128,128]{2,1,0:T(8,128)S(1)} %get-tuple-element.71), custom_call_target="InvertDiagBlocksLowerTriangular" | custom-call | tf_op jit(solution)/shard_map/jit(cholesky)/cholesky | solution.py:125
  407.7 11.7 %cholesky.181 = f32[128,128]{1,0:T(8,128)S(1)} custom-call(f32[128,128]{1,0:T(8,128)S(1)} %convolution_subtract_fusion.2), custom_call_target="Cholesky" | custom-call | tf_op jit(solution)/shard_map/jit(cholesky)/cholesky | solution.py:125
  419.4 3.1 all-reduce.14.cloned.1.call-done
  422.5 2.5 copy.67
  427.7 4.3 while.6
  432.1 19.7 %custom-call.38 = f32[2,128,128]{1,2,0:T(8,128)S(1)} custom-call(f32[2,128,128]{2,1,0:T(8,128)S(1)} %get-tuple-element.27), custom_call_target="InvertDiagBlocksLowerTriangular" | custom-call | tf_op jit(solution)/shard_map/triangular_solve/custom-call.5 | solution.py:47
  451.8 51.4 %all-reduce.16.cloned.1.call-done = f32[256,1024]{0,1:T(8,128)} async-done(((f32[256,1024]{0,1:T(8,128)}), f32[256,1024]{0,1:T(8,128)}) %all-reduce.16.cloned.1.call-update) | async-done | bytes 1048592 | tf_op jit(solution)/shard_map/psum | solution.py:124
  503.2 1.7 fusion.26
  504.8 2.0 convolution_subtract_fusion.1
  (145 shorter events, 63.6 us)
Async XLA Ops:
  8.0 81.8 %copy-start = (bf16[4,256,256]{2,1,0:T(8,128)(2,1)S(1)}, bf16[4,256,256]{2,1,0:T(8,128)(2,1)}, u32[]{:S(2)}) copy-start(bf16[4,256,256]{2,1,0:T(8,128)(2,1)} %param.10) | copy-start | bytes 1572868
  8.0 143.6 %all-reduce.10.cloned.1.call-start = ((), (), s32[]{:S(2)}) async-start(), calls=%async_computation.2 | async-start | bytes 524288 | tf_op jit(solution)/shard_map/psum | solution.py:60
  9.9 206.4 %reduce-scatter.3.cloned.1.call-start = ((), (), s32[]{:S(2)}) async-start(), calls=%async_computation.3 | async-start | bytes 2621440 | tf_op jit(solution)/shard_map/reduce_scatter | solution.py:79
  50.7 1.8 copy-start.4
  50.8 2.0 copy-start.6
  52.6 1.7 copy-start.7
  59.0 3.1 copy-start.3
  82.9 0.8 copy-start.9
  82.9 134.6 %reduce-scatter.5.cloned.1.call-start = ((), (), s32[]{:S(2)}) async-start(), calls=%async_computation.4 | async-start | bytes 1179648 | tf_op jit(solution)/shard_map/reduce_scatter | solution.py:99
  119.8 3.1 copy-start.2
  127.9 1.0 copy-start.1
  128.9 254.7 %all-reduce.12.cloned.1.call-start = ((), (), s32[]{:S(2)}) async-start(), calls=%async_computation.5 | async-start | bytes 524288 | tf_op jit(solution)/shard_map/psum | solution.py:123
  151.7 2.5 copy-start.8
  261.1 161.5 %all-reduce.14.cloned.1.call-start = ((), (), s32[]{:S(2)}) async-start(), calls=%async_computation.6 | async-start | bytes 2097152 | tf_op jit(solution)/shard_map/psum | solution.py:124
  264.3 3.0 copy-start.5
  278.6 224.5 %all-reduce.16.cloned.1.call-start = ((), (), s32[]{:S(2)}) async-start(), calls=%async_computation.7 | async-start | bytes 2097152 | tf_op jit(solution)/shard_map/psum | solution.py:124
Sparse Core Ops, SparseCore 0:
  14.3 137.2 all-reduce.9
  261.2 122.3 all-reduce.11
  386.5 35.9 all-reduce.13
Sparse Core Ops, SparseCore 1:
  83.0 32.4 reduce-scatter.2
  129.0 64.7 reduce-scatter.4
  425.2 77.9 all-reduce.15
